TPU v7x, 128 devices: a whole 4x4x4 slice. The times are simulated.
128 devices in a mesh: seq: 16 (over y, z), batch: 8 (over x, core).
Axes of the slice: x: 4, y: 4, z: 4, core: 2. Of those that a mesh axis runs over, the one named last changes fastest.
Arguments:
- q_nope: bfloat16 [8, 64, 128, 128], P('batch', None, 'seq'), may hold values from -6 to 6
- q_rope: bfloat16 [8, 64, 128, 64], P('batch', None, 'seq'), may hold values from -8 to 8
- absorb_k: bfloat16 [128, 128, 512], P('seq'), may hold values from -0.5 to 0.5
- absorb_v: bfloat16 [128, 512, 128], P('seq'), may hold values from -0.25 to 0.25
- cache_latent: bfloat16 [8, 16384, 512], P('batch', 'seq'), may hold values from -6 to 6
- cache_rope: bfloat16 [8, 16384, 64], P('batch', 'seq'), may hold values from -8 to 8
- draft_latent: bfloat16 [8, 64, 512], P('batch'), may hold values from -6 to 6
- draft_rope: bfloat16 [8, 64, 64], P('batch'), may hold values from -6 to 6
- residual: bfloat16 [512, 7168], P('batch', 'seq'), may hold values from -1.2 to 1.2
- out_proj: bfloat16 [16384, 7168], P('seq'), may hold values from -0.046875 to 0.046875
- norm_gain: float32 [7168], replicated, may hold values from 0.5 to 1.5
- lm_head: bfloat16 [65536, 7168], P(('seq', 'batch')), may hold values from -2.4095235 to 2.4095235
- parent: int32 [8, 64], replicated, may hold values from 0 to 62, as said below
- draft_ids: int32 [8, 64], replicated, may hold values from 0 to 65535
- cache_len: int32 [8], P('batch'), may hold values from 4096 to 16384
- accept_len: int32 [8], P('batch'), may hold values from 1 to 64
Outputs:
- hidden_out: bfloat16 [512, 7168], P('batch', 'seq')
- target_logp: float32 [8, 64], P('batch')
- accepted_score: float32 [8], P('batch')
Inputs may be any that keep to these rules, and one draw needn't show every extreme that they name: parent[b, 0] = 0, and 0 <= parent[b, i] < i for i >= 1.
All inputs are finite; a program needn't handle non-finite values.
Results may differ from a plain program's by a relative error of at most 0.0095.
Values may be sent and summed in bfloat16 or wider, within the bound.
A program may use at most 256 MiB of HBM per device.

v0:
```python
import math
import jax
import jax.numpy as jnp
from jax import lax
from jax.sharding import Mesh
from jax.sharding import PartitionSpec as P

SEQ = ("seq_0", "seq_1")
BATCH = ("batch_0", "batch_1")
SEQ_BATCH = ("seq_0", "seq_1", "batch_0", "batch_1")
masked_value = -1e30
norm_epsilon = 1e-06
highest = lax.Precision.HIGHEST


def sent_together(arrays, axis, dim, along):
    ends, at = ([], 0)
    for a in arrays[:-1]:
        at += a.shape[along]
        ends.append(at)
    both = jnp.concatenate(arrays, axis=along)
    return tuple(jnp.split(lax.all_gather(both, axis, axis=dim, tiled=True), ends, axis=along))


def copy_for_each(array, axis):
    copies = jnp.broadcast_to(array, (lax.axis_size(axis), *array.shape))
    return lax.all_to_all(copies, axis, split_axis=0, concat_axis=0, tiled=True)


def over_copies(array, axis):
    everything = copy_for_each(array, axis)
    return jnp.max(everything, axis=0)


def gathered_once(array, axis):
    leaves = jax.tree.leaves(array)
    sequence = sorted(range(len(leaves)), key=lambda k: -leaves[k].size)
    width = (1, *leaves[sequence[0]].shape)[-1]
    lines = [
        jnp.pad(leaves[k].reshape(-1), (0, -leaves[k].size % width)).reshape(-1, width)
        for k in sequence
    ]
    both, at, found = (lax.all_gather(jnp.concatenate(lines), axis), 0, {})
    for k, line in zip(sequence, lines):
        piece = both[:, at : at + len(line)].reshape(len(both), -1)
        found[k] = piece[:, : leaves[k].size].reshape(-1, *leaves[k].shape)
        at += len(line)
    numbers = iter(range(len(leaves)))
    return jax.tree.map(lambda _: found[next(numbers)], array)


def combined_by_axis(array, axes, combine):
    for axis in axes:
        pieces = gathered_once(array, axis)
        array = jax.tree.map(lambda part: part[0], pieces)
        for k in range(1, lax.axis_size(axis)):
            array = combine(array, jax.tree.map(lambda part: part[k], pieces))
    return array


def ancestry_of(parents):
    draft_count = parents.shape[1]
    indices = jnp.arange(draft_count, dtype=jnp.int32)
    parent_map = (
        (parents[:, :, None] == indices[None, None, :]) & (indices[None, :, None] > 0)
    ).astype(jnp.float32)
    ancestry = jnp.broadcast_to(jnp.eye(draft_count, dtype=jnp.float32), parent_map.shape)
    for doubling in range(draft_count.bit_length() - 1):
        ancestry = ancestry + jnp.einsum("rij,rjk->rik", ancestry, parent_map, precision=highest)
        parent_map = jnp.einsum("rij,rjk->rik", parent_map, parent_map, precision=highest)
    return ancestry > 0.5


def combine_soft(earlier, later):
    top_new = jnp.maximum(earlier[0], later[0])
    mass_new = earlier[1] * jnp.exp(earlier[0] - top_new) + later[1] * jnp.exp(later[0] - top_new)
    return (top_new, mass_new, earlier[2] + later[2])


def body(
    q_nope,
    q_rope,
    absorb_k,
    absorb_v,
    cache_latent,
    cache_rope,
    draft_latent,
    draft_rope,
    residual,
    out_proj,
    norm_gain,
    lm_head,
    parent,
    draft_ids,
    cache_len,
    accept_len,
):
    requests, draft_count, local_heads, nope_width = q_nope.shape
    cache_rows = cache_latent.shape[1]
    score_scale = 1.0 / math.sqrt(nope_width + q_rope.shape[3])
    seq_index = lax.axis_index(SEQ)
    batch_index = lax.axis_index(BATCH)
    query_latent = jnp.einsum(
        "rihn,hnc->rihc", q_nope, absorb_k, preferred_element_type=jnp.float32
    ).astype(jnp.bfloat16)
    query_all, rope_all = sent_together((query_latent, q_rope), SEQ, 2, 3)
    cache_scores = jnp.einsum(
        "rihc,rtc->rhit", query_all, cache_latent, preferred_element_type=jnp.float32
    )
    cache_scores = cache_scores + jnp.einsum(
        "rihe,rte->rhit", rope_all, cache_rope, preferred_element_type=jnp.float32
    )
    positions = seq_index * cache_rows + jnp.arange(cache_rows, dtype=jnp.int32)
    in_cache = positions[None, :] < cache_len[:, None]
    cache_scores = jnp.where(in_cache[:, None, None, :], cache_scores * score_scale, masked_value)
    tree_scores = jnp.einsum(
        "rihc,rjc->rhij", query_all, draft_latent, preferred_element_type=jnp.float32
    )
    tree_scores = tree_scores + jnp.einsum(
        "rihe,rje->rhij", rope_all, draft_rope, preferred_element_type=jnp.float32
    )
    own_parents = lax.dynamic_slice_in_dim(parent, batch_index * requests, requests, 0)
    ancestry = ancestry_of(own_parents)
    tree_scores = jnp.where(ancestry[:, None, :, :], tree_scores * score_scale, masked_value)
    local_top = jnp.maximum(jnp.max(cache_scores, axis=3), jnp.max(tree_scores, axis=3))
    row_top = over_copies(local_top, SEQ)
    cache_weights = jnp.exp(cache_scores - row_top[..., None])
    weight_sum = jnp.sum(cache_weights, axis=3)
    partial_value = jnp.einsum(
        "rhit,rtc->rhic",
        cache_weights.astype(jnp.bfloat16),
        cache_latent,
        preferred_element_type=jnp.float32,
    )
    head_first = seq_index * local_heads
    tree_mine = lax.dynamic_slice_in_dim(tree_scores, head_first, local_heads, 1)
    top_mine = lax.dynamic_slice_in_dim(row_top, head_first, local_heads, 1)
    tree_weights = jnp.exp(tree_mine - top_mine[..., None])
    tree_out = jnp.einsum(
        "rhij,rjc->rhic",
        tree_weights.astype(jnp.bfloat16),
        draft_latent,
        preferred_element_type=jnp.float32,
    )
    latent_sum, weight_total = (
        lax.psum_scatter(partial_value, SEQ, scatter_dimension=1, tiled=True),
        lax.psum_scatter(weight_sum, SEQ, scatter_dimension=1, tiled=True),
    )
    summed = jnp.einsum(
        "rhic,hcn->rhin", latent_sum + tree_out, absorb_v, preferred_element_type=jnp.float32
    )
    weight_total = weight_total + jnp.sum(tree_weights, axis=3)
    head_out = (summed / weight_total[..., None]).astype(jnp.bfloat16)
    head_rows = jnp.transpose(head_out, (0, 2, 1, 3)).reshape(
        requests * draft_count, local_heads * head_out.shape[3]
    )
    branch_term = jnp.dot(head_rows, out_proj, preferred_element_type=jnp.float32)
    width_local = residual.shape[1]
    feature_first = seq_index * width_local
    residual_wide = lax.dynamic_update_slice_in_dim(
        jnp.zeros_like(branch_term), residual.astype(jnp.float32), feature_first, 1
    )
    stream = lax.psum(branch_term + residual_wide, SEQ)
    square = jnp.sum(stream * stream, axis=1)
    normed = (
        stream * lax.rsqrt(square / stream.shape[1] + norm_epsilon)[:, None] * norm_gain
    ).astype(jnp.bfloat16)
    hidden_out = lax.dynamic_slice_in_dim(stream, feature_first, width_local, 1).astype(
        jnp.bfloat16
    )
    vocab_rows = lm_head.shape[0]
    vocab_first = lax.axis_index(SEQ_BATCH) * vocab_rows
    logits = jnp.einsum(
        "rd,vd->rv",
        lax.all_gather(normed, BATCH, axis=0, tiled=True),
        lm_head,
        preferred_element_type=jnp.float32,
    )
    request_total = parent.shape[0]
    parent_rows = (
        jnp.arange(request_total, dtype=jnp.int32)[:, None] * draft_count + parent
    ).reshape(-1)
    source = logits[parent_rows]
    column = jnp.arange(vocab_rows, dtype=jnp.int32) + vocab_first
    picked = jnp.sum(
        jnp.where(column[None, :] == draft_ids.reshape(-1)[:, None], source, 0.0), axis=1
    )
    local_best = jnp.max(logits, axis=1)
    local_mass = jnp.sum(jnp.exp(logits - local_best[:, None]), axis=1)
    best, exp_mass, chosen = combined_by_axis(
        (local_best, local_mass, picked), SEQ_BATCH, combine_soft
    )
    log_total = best + jnp.log(exp_mass)
    target_all = (chosen - log_total[parent_rows]).reshape(request_total, draft_count)
    target_logp = lax.dynamic_slice_in_dim(target_all, batch_index * requests, requests, 0)
    accepted_score = jnp.sum(
        jnp.where(
            jnp.arange(draft_count, dtype=jnp.int32)[None, :] < accept_len[:, None],
            target_logp,
            0.0,
        ),
        axis=1,
    )
    return (hidden_out, target_logp, accepted_score)


def solution(mesh):
    split = Mesh(mesh.devices.reshape(4, 4, 4, 2), ("seq_0", "seq_1", "batch_0", "batch_1"))
    in_specs = (
        P(BATCH, None, SEQ, None),
        P(BATCH, None, SEQ, None),
        P(SEQ, None, None),
        P(SEQ, None, None),
        P(BATCH, SEQ, None),
        P(BATCH, SEQ, None),
        P(BATCH, None, None),
        P(BATCH, None, None),
        P(BATCH, SEQ),
        P(SEQ, None),
        P(),
        P(SEQ_BATCH, None),
        P(),
        P(),
        P(BATCH),
        P(BATCH),
    )
    out_specs = (P(BATCH, SEQ), P(BATCH, None), P(BATCH))
    return jax.shard_map(body, mesh=split, in_specs=in_specs, out_specs=out_specs, check_vma=False)
```

profile of v0, /device:TPU:1, one launch (start us, length us, event | category | flops | bytes accessed | tf_op | source)
XLA Modules:
  0.0 529.6 jit_solution(17929896783594325636)
XLA Ops:
  7.2 1.0 copy.41
  8.2 1.6 fusion.16
  9.9 0.9 maximum_bitcast_fusion
  11.5 0.7 fusion.88
  12.2 0.2 fusion.39
  12.5 0.2 convolution_add_fusion.5
  12.7 0.2 fusion.99
  12.8 0.2 convolution_add_fusion.4
  13.0 0.2 fusion.100
  13.2 0.2 convolution_add_fusion.3
  13.3 0.2 fusion.101
  13.5 0.2 convolution_add_fusion.2
  13.7 0.2 fusion.102
  13.9 0.2 convolution_add_fusion.1
  14.0 0.2 fusion.17
  14.2 0.1 copy.45
  14.3 80.4 %all-gather.11.cloned.1.call-done = bf16[1,64,128,576]{3,1,0,2:T(8,128)(2,1)} async-done(((bf16[1,64,8,576]{3,1,0,2:T(8,128)(2,1)}), bf16[1,64,128,576]{3,1,0,2:T(8,128)(2,1)}) %all-gather.11.cloned.1.call-update) | async-done | bytes 9437200 | tf_op jit(solution)/shard_map/all_gather | solution.py:22
  94.7 1.8 split.9
  96.5 2.9 copy.69
  99.4 7.5 %fusion.10 = f32[64,128,64]{0,2,1:T(8,128)S(1)} fusion(bf16[1,64,512]{2,1,0:T(8,128)(2,1)S(1)} %copy-done.5, bf16[1,64,128,576]{3,1,0,2:T(8,128)(2,1)} %all-gather.11.cloned.1.call-done), kind=kOutput, calls=%fused_computation.11 | convolution fusion | flops 536870912 | bytes 10551296 | tf_op jit(solution)/shard_map/rihc,rjc->rhij/dot_general | solution.py:116
  106.9 5.8 %fusion.97 = (f32[128,64]{1,0:T(8,128)S(1)}, f32[1,128,64,64]{2,3,1,0:T(8,128)}) fusion(f32[64,128,64]{0,2,1:T(8,128)S(1)} %fusion.10, bf16[1,64,64]{2,1,0:T(8,128)(2,1)S(1)} %copy-done.8, bf16[1,64,128,576]{3,1,0,2:T(8,128)(2,1)} %all-gather.11.cloned.1.call-done, pred[64,64]{0,1:T(8,128)(4,1)S(1)} %copy.45), kind=kOutput, calls=%fused_computation.169 | convolution fusion | flops 69197824 | bytes 6336512 | tf_op jit(solution)/shard_map/rihe,rje->rhij/dot_general | solution.py:119
  112.8 7.7 %split.8 = bf16[1,64,128,512]{3,1,0,2:T(8,128)(2,1)} slice(bf16[1,64,128,576]{3,1,0,2:T(8,128)(2,1)} %all-gather.11.cloned.1.call-done), slice={[0:1], [0:64], [0:128], [0:512]} | slice | bytes 16777216 | tf_op jit(solution)/shard_map/split | solution.py:22
  120.5 30.0 %fusion.12 = f32[64,128,1024]{2,1,0:T(8,128)} fusion(bf16[1,64,128,512]{3,1,0,2:T(8,128)(2,1)} %split.8, bf16[1,1024,512]{2,1,0:T(8,128)(2,1)S(1)} %copy-done), kind=kOutput, calls=%fused_computation.14 | convolution fusion | flops 8589934592 | bytes 42991616 | tf_op jit(solution)/shard_map/rihc,rtc->rhit/dot_general | solution.py:107
  150.5 21.9 %fusion.96 = (f32[128,64]{0,1:T(8,128)S(1)}, f32[1,128,64,1024]{3,1,2,0:T(8,128)}) fusion(f32[64,128,1024]{2,1,0:T(8,128)} %fusion.12, bf16[1,1024,64]{1,2,0:T(8,128)(2,1)S(1)} %copy-done.4, bf16[1,64,128,64]{2,3,1,0:T(8,128)(2,1)S(1)} %copy-done.3, pred[1024]{0:T(1024)(128)(4,1)S(1)} %add_compare_fusion), kind=kOutput, calls=%fused_computation.168 | convolution fusion | flops 1107288064 | bytes 68322304 | tf_op jit(solution)/shard_map/rihe,rte->rhit/dot_general | solution.py:110
  172.5 15.1 %all_to_all.5 = f32[16,1,128,64]{2,3,1,0:T(8,128)S(1)} all-to-all(f32[16,1,128,64]{2,3,1,0:T(8,128)S(1)} %broadcast_in_dim.37), channel_id=1, replica_groups=mesh['seq_0'=4,'seq_1'=4,'batch_0'=4,'batch_1'=2] {'seq_0','seq_1'}, dimensions={0} | all-to-all | bytes 1048576 | tf_op jit(solution)/shard_map/all_to_all | solution.py:27
  187.7 18.7 %fusion.7 = f32[1,128,64,512]{3,1,2,0:T(8,128)} fusion(f32[1,128,64,1024]{3,1,2,0:T(8,128)} %get-tuple-element.19, f32[128,64]{0,1:T(8,128)S(1)} %reduce_max.38, bf16[1,1024,512]{2,1,0:T(8,128)(2,1)S(1)} %copy-done), kind=kOutput, calls=%fused_computation.10 | convolution fusion | flops 8606711808 | bytes 51412992 | tf_op jit(solution)/shard_map/rhit,rtc->rhic/dot_general | solution.py:129
  206.5 0.6 copy-done.12
  207.0 0.6 dynamic-slice.5
  208.3 0.1 constant_dynamic-slice_fusion.1
  208.4 1.0 fusion.24
  209.4 0.1 copy.67
  209.5 14.9 %fusion.1 = f32[128,64]{0,1:T(8,128)S(1)} fusion(f32[1,128,64,1024]{3,1,2,0:T(8,128)} %get-tuple-element.19, f32[128,64]{0,1:T(8,128)S(1)} %reduce_max.38), kind=kLoop, calls=%fused_computation.5 | loop fusion | flops 16769024 | bytes 33619968 | tf_op jit(solution)/shard_map/reduce_sum | solution.py:128
  224.5 0.1 copy.53
  224.6 58.5 %all-reduce = f32[1,128,64]{2,1,0:T(8,128)S(1)} all-reduce(f32[1,128,64]{2,1,0:T(8,128)S(1)} %copy.53), channel_id=7, replica_groups=mesh['seq_0'=4,'seq_1'=4,'batch_0'=4,'batch_1'=2] {'seq_0','seq_1'}, use_global_device_ids=true, to_apply=%region_5.6.clone | all-reduce | flops 8192 | bytes 65536
  283.1 0.1 copy.55
  283.2 0.1 copy.61
  283.4 33.9 %reduce-scatter.3.cloned.1.call-done = f32[1,8,64,512]{3,1,2,0:T(8,128)} async-done(((f32[1,128,64,512]{3,1,2,0:T(8,128)}), f32[1,8,64,512]{3,1,2,0:T(8,128)}) %reduce-scatter.3.cloned.1.call-update) | async-done | bytes 1048592 | tf_op jit(solution)/shard_map/reduce_scatter | solution.py:146
  317.3 1.5 fusion.15
  318.9 0.4 fusion.19
  319.2 0.1 copy.57
  319.4 7.9 %fusion.27 = f32[64,7168]{1,0:T(8,128)S(1)} fusion(bf16[1024,7168]{1,0:T(8,128)(2,1)} %param.25, bf16[8,8,8,128]{3,2,1,0:T(8,128)(2,1)S(1)} %bitcast.377), kind=kOutput, calls=%fused_computation.45 | convolution fusion | flops 939524096 | bytes 16646144 | tf_op jit(solution)/shard_map/dot_general | solution.py:157
  327.2 0.1 convert_add_fusion
  327.4 1.1 add.352
  328.5 1.2 copy-done.2
  329.8 88.2 %all-reduce.3.cloned.1.call-done = f32[64,7168]{1,0:T(8,128)} async-done(((f32[64,7168]{1,0:T(8,128)}), f32[64,7168]{1,0:T(8,128)}) %all-reduce.3.cloned.1.call-update) | async-done | bytes 1835024 | tf_op jit(solution)/shard_map/psum | solution.py:163
  418.0 1.7 multiply_reduce_fusion
  419.7 2.7 multiply_convert_fusion
  423.1 0.1 eq.74
  423.2 0.1 reshape.1086
  423.3 1.6 dynamic-slice_convert_fusion
  425.0 43.8 %all-gather.13.cloned.1.call-done = bf16[512,7168]{1,0:T(8,128)(2,1)} async-done(((bf16[64,7168]{1,0:T(8,128)(2,1)}), bf16[512,7168]{1,0:T(8,128)(2,1)}) %all-gather.13.cloned.1.call-update) | async-done | bytes 7340048 | tf_op jit(solution)/shard_map/all_gather | solution.py:175
  468.8 8.5 %fusion.98 = (f32[512]{0:T(512)S(1)}, f32[512,512]{0,1:T(8,128)S(1)}) fusion(bf16[512,7168]{1,0:T(8,128)(2,1)} %all-gather.13.cloned.1.call-done, bf16[512,7168]{1,0:T(8,128)(2,1)} %param.27), kind=kOutput, calls=%fused_computation.170 | convolution fusion | flops 3758358016 | bytes 15730688 | tf_op jit(solution)/shard_map/rd,vd->rv/dot_general | solution.py:173
  477.3 0.3 copy.58
  477.6 0.2 exponential_reduce_fusion
  477.8 1.6 gather_fusion
  479.5 0.3 select_reduce_fusion
  479.7 9.6 %all-gather.4 = f32[4,3,512]{2,1,0:T(4,128)S(1)} all-gather(f32[1,3,512]{2,1,0:T(4,128)S(1)} %maximum_bitcast_fusion.1), channel_id=2, replica_groups=mesh['seq_0'=4,'seq_1'=4,'batch_0'=4,'batch_1'=2] {'seq_0'}, dimensions={0}, use_global_device_ids=true | all-gather | bytes 30720 | tf_op jit(solution)/shard_map/all_gather | solution.py:43
  489.4 9.5 %all-gather.5 = f32[4,3,512]{2,1,0:T(4,128)S(1)} all-gather(f32[1,3,512]{2,1,0:T(4,128)S(1)} %maximum_bitcast_fusion.2), channel_id=3, replica_groups=mesh['seq_0'=4,'seq_1'=4,'batch_0'=4,'batch_1'=2] {'seq_1'}, dimensions={0}, use_global_device_ids=true | all-gather | bytes 30720 | tf_op jit(solution)/shard_map/all_gather | solution.py:43
  498.9 9.0 %all-gather.6 = f32[4,3,512]{2,1,0:T(4,128)S(1)} all-gather(f32[1,3,512]{2,1,0:T(4,128)S(1)} %maximum_bitcast_fusion.3), channel_id=4, replica_groups=mesh['seq_0'=4,'seq_1'=4,'batch_0'=4,'batch_1'=2] {'batch_0'}, dimensions={0}, use_global_device_ids=true | all-gather | bytes 30720 | tf_op jit(solution)/shard_map/all_gather | solution.py:43
  508.0 10.2 %all-gather.7 = f32[2,3,512]{2,1,0:T(4,128)S(1)} all-gather(f32[1,3,512]{2,1,0:T(4,128)S(1)} %maximum_bitcast_fusion.4), channel_id=5, replica_groups=mesh['seq_0'=4,'seq_1'=4,'batch_0'=4,'batch_1'=2] {'batch_1'}, dimensions={0}, use_global_device_ids=true | all-gather | bytes 18432 | tf_op jit(solution)/shard_map/all_gather | solution.py:43
  518.3 3.5 gather_fusion.1
  521.8 0.1 gather.10
  521.8 0.1 add.384
  521.9 1.1 fusion.89
  (61 shorter events, 0.9 us)
Async XLA Ops:
  7.2 113.3 %copy-start = (bf16[1,1024,512]{2,1,0:T(8,128)(2,1)S(1)}, bf16[1,1024,512]{2,1,0:T(8,128)(2,1)}, u32[]{:S(2)}) copy-start(bf16[1,1024,512]{2,1,0:T(8,128)(2,1)} %param.20) | copy-start | bytes 3145732
  7.2 92.3 %copy-start.5 = (bf16[1,64,512]{2,1,0:T(8,128)(2,1)S(1)}, bf16[1,64,512]{2,1,0:T(8,128)(2,1)}, u32[]{:S(2)}) copy-start(bf16[1,64,512]{2,1,0:T(8,128)(2,1)} %param.22) | copy-start | bytes 196612
  7.2 87.5 %all-gather.11.cloned.1.call-start = ((), (), s32[]{:S(2)}) async-start(), calls=%async_computation.2 | async-start | bytes 11141120 | tf_op jit(solution)/shard_map/all_gather | solution.py:22
  10.8 306.5 %reduce-scatter.3.cloned.1.call-start = ((), (), s32[]{:S(2)}) async-start(), calls=%async_computation.3 | async-start | bytes 17825792 | tf_op jit(solution)/shard_map/reduce_scatter | solution.py:146
  96.5 10.4 %copy-start.8 = (bf16[1,64,64]{2,1,0:T(8,128)(2,1)S(1)}, bf16[1,64,64]{2,1,0:T(8,128)(2,1)}, u32[]{:S(2)}) copy-start(bf16[1,64,64]{2,1,0:T(8,128)(2,1)} %param.23) | copy-start | bytes 24580
  120.5 30.0 %copy-start.3 = (bf16[1,64,128,64]{2,3,1,0:T(8,128)(2,1)S(1)}, bf16[1,64,128,64]{2,3,1,0:T(8,128)(2,1)}, u32[]{:S(2)}) copy-start(bf16[1,64,128,64]{2,3,1,0:T(8,128)(2,1)} %copy.69) | copy-start | bytes 3145732
  120.5 30.0 %copy-start.4 = (bf16[1,1024,64]{1,2,0:T(8,128)(2,1)S(1)}, bf16[1,1024,64]{1,2,0:T(8,128)(2,1)}, u32[]{:S(2)}) copy-start(bf16[1,1024,64]{1,2,0:T(8,128)(2,1)} %param.21) | copy-start | bytes 393220
  206.4 0.7 copy-start.12
  206.4 211.5 %all-reduce.3.cloned.1.call-start = ((), (), s32[]{:S(2)}) async-start(), calls=%async_computation.4 | async-start | bytes 3670016 | tf_op jit(solution)/shard_map/psum | solution.py:163
  209.5 109.3 %copy-start.11 = (bf16[8,512,128]{2,1,0:T(8,128)(2,1)S(1)}, bf16[8,512,128]{2,1,0:T(8,128)(2,1)}, u32[]{:S(2)}) copy-start(bf16[8,512,128]{2,1,0:T(8,128)(2,1)} %param.19) | copy-start | bytes 3145732
  319.3 7.9 %copy-start.6 = (bf16[64,448]{1,0:T(8,128)(2,1)S(1)}, bf16[64,448]{1,0:T(8,128)(2,1)}, u32[]{:S(2)}) copy-start(bf16[64,448]{1,0:T(8,128)(2,1)} %param.24) | copy-start | bytes 172036
  319.3 100.3 %copy-start.7 = (f32[7168]{0:T(1024)S(1)}, f32[7168]{0:T(1024)}, u32[]{:S(2)}) copy-start(f32[7168]{0:T(1024)} %param.26) | copy-start | bytes 86020
  319.4 103.7 %copy-start.9 = (s32[8,64]{1,0:T(8,128)S(1)}, s32[8,64]{1,0:T(8,128)}, u32[]{:S(2)}) copy-start(s32[8,64]{1,0:T(8,128)} %param.29) | copy-start | bytes 6148
  319.4 103.8 %copy-start.10 = (s32[8,64]{1,0:T(8,128)S(1)}, s32[8,64]{1,0:T(8,128)}, u32[]{:S(2)}) copy-start(s32[8,64]{1,0:T(8,128)} %param.28) | copy-start | bytes 6148
  328.5 1.3 copy-start.2
  329.7 139.0 %all-gather.13.cloned.1.call-start = ((), (), s32[]{:S(2)}) async-start(), calls=%async_computation.5 | async-start | bytes 8257536 | tf_op jit(solution)/shard_map/all_gather | solution.py:175
  468.8 54.3 %copy-start.1 = (bf16[1,1024,512]{2,1,0:T(8,128)(2,1)S(1)}, bf16[1,1024,512]{2,1,0:T(8,128)(2,1)}, u32[]{:S(2)}) copy-start(bf16[1,1024,512]{2,1,0:T(8,128)(2,1)} %param.20) | copy-start | bytes 3145732
Sparse Core Ops, SparseCore 0:
  10.9 83.7 all-gather.10
  206.5 110.7 reduce-scatter.2
  329.9 88.0 all-reduce.2
  422.5 46.2 all-gather.12
where the time goes:
time: 530 us
  waiting for transfers between devices  246 us (46%)
  blocking collectives  112 us (21%)
  matrix products  106 us (20%)
  local copies, waits for them, and re-layouts  26 us (5%)
  other arithmetic  23.3 us (4%)
  between operations  16.1 us (3%)
    psum x1, waiting for transfers between devices, body(): stream = lax.psum(branch_term + residual_wide, SEQ)  88.2 us
    all_gather x1, waiting for transfers between devices, sent_together(): lax.all_gather(both, axis, axis=dim, tiled=True)  80.4 us
    unnamed x1, blocking collectives  58.5 us
    all_gather x1, waiting for transfers between devices, body(): lax.all_gather(normed, BATCH, axis=0, tiled=True)  43.8 us
    all_gather x4, blocking collectives, gathered_once(): both, at, found = (lax.all_gather(jnp.concatenate(lines), axis), 0, {})  38.3 us
    reduce_scatter x1, waiting for transfers between devices, body(): lax.psum_scatter(partial_value, SEQ, scatter_dimension=1, tiled=True)  33.9 us
    dot_general x1, matrix products, body(): jnp.einsum('rihc,rtc->rhit', query_all, cache_latent, preferred_element_t...  30 us
    dot_general x1, matrix products, body(): jnp.einsum('rihe,rte->rhit', rope_all, cache_rope, preferred_element_type...  21.9 us
  transfers between devices with their start and end apart: 4, of which 4 were waited for; matrix products, arithmetic and copies ran while one was open for 4% of the time, Pallas kernels for 0%

commit v1 on v0

--- a/solution.py
+++ b/solution.py
@@ -172,7 +172,9 @@
     vocab_first = lax.axis_index(SEQ_BATCH) * vocab_rows
     logits = jnp.einsum(
         "rd,vd->rv",
-        lax.all_gather(normed, BATCH, axis=0, tiled=True),
+        jnp.concatenate(
+            lax.all_to_all(jnp.stack([normed] * lax.axis_size(BATCH)), BATCH, 0, 0), axis=0
+        ),
         lm_head,
         preferred_element_type=jnp.float32,
     )

time: 530 us -> 576 us (1.087)
  waiting for transfers between devices: 246 us -> 283 us
  starting transfers between devices: 0.16 us -> 6.97 us
    all_to_all x0 -> x1, waiting for transfers between devices: none -> 80.1 us  [body(): lax.all_to_all(jnp.stack([normed] * lax.axis_size(BATCH)), BATCH, 0, 0)]
    all_gather x1 -> x0, waiting for transfers between devices: 43.8 us -> none  [body(): lax.all_gather(normed, BATCH, axis=0, tiled=True)]
    all_to_all x0 -> x1, starting transfers between devices: none -> 6.85 us  [body(): lax.all_to_all(jnp.stack([normed] * lax.axis_size(BATCH)), BATCH, 0, 0)]
where the time goes in v1:
time: 576 us; the launch traced here: 575 us
  waiting for transfers between devices  283 us (49%)
  blocking collectives  112 us (19%)
  matrix products  106 us (18%)
  local copies, waits for them, and re-layouts  29.9 us (5%)
  other arithmetic  22.4 us (4%)
  between operations  16.1 us (3%)
  starting transfers between devices  6.97 us (1%)
    psum x1, waiting for transfers between devices, body(): stream = lax.psum(branch_term + residual_wide, SEQ)  88.1 us
    all_gather x1, waiting for transfers between devices, sent_together(): lax.all_gather(both, axis, axis=dim, tiled=True)  80.4 us
    all_to_all x1, waiting for transfers between devices, body(): lax.all_to_all(jnp.stack([normed] * lax.axis_size(BATCH)), BATCH, 0, 0)  80.1 us
    unnamed x1, blocking collectives  58.5 us
    all_gather x4, blocking collectives, gathered_once(): both, at, found = (lax.all_gather(jnp.concatenate(lines), axis), 0, {})  38.1 us
    reduce_scatter x1, waiting for transfers between devices, body(): lax.psum_scatter(partial_value, SEQ, scatter_dimension=1, tiled=True)  34 us
    dot_general x1, matrix products, body(): jnp.einsum('rihc,rtc->rhit', query_all, cache_latent, preferred_element_t...  30 us
    dot_general x1, matrix products, body(): jnp.einsum('rihe,rte->rhit', rope_all, cache_rope, preferred_element_type...  21.9 us
  transfers between devices with their start and end apart: 4, of which 4 were waited for; matrix products, arithmetic and copies ran while one was open for 4% of the time, Pallas kernels for 0%

profile of v1, /device:TPU:1, one launch (start us, length us, event | category | flops | bytes accessed | tf_op | source)
XLA Modules:
  0.0 575.4 jit_solution(11403676779518332142)
XLA Ops:
  7.2 1.0 copy.41
  8.2 1.6 fusion.16
  9.9 0.9 maximum_bitcast_fusion
  11.5 0.7 fusion.88
  12.2 0.2 fusion.39
  12.5 0.2 convolution_add_fusion.5
  12.7 0.2 fusion.99
  12.8 0.2 convolution_add_fusion.4
  13.0 0.2 fusion.100
  13.2 0.2 convolution_add_fusion.3
  13.3 0.2 fusion.101
  13.5 0.2 convolution_add_fusion.2
  13.7 0.2 fusion.102
  13.9 0.2 convolution_add_fusion.1
  14.0 0.2 fusion.17
  14.2 0.1 copy.45
  14.3 80.4 %all-gather.10.cloned.1.call-done = bf16[1,64,128,576]{3,1,0,2:T(8,128)(2,1)} async-done(((bf16[1,64,8,576]{3,1,0,2:T(8,128)(2,1)}), bf16[1,64,128,576]{3,1,0,2:T(8,128)(2,1)}) %all-gather.10.cloned.1.call-update) | async-done | bytes 9437200 | tf_op jit(solution)/shard_map/all_gather | solution.py:22
  94.7 1.8 split.9
  96.5 2.9 copy.69
  99.4 7.5 %fusion.10 = f32[64,128,64]{0,2,1:T(8,128)S(1)} fusion(bf16[1,64,512]{2,1,0:T(8,128)(2,1)S(1)} %copy-done.5, bf16[1,64,128,576]{3,1,0,2:T(8,128)(2,1)} %all-gather.10.cloned.1.call-done), kind=kOutput, calls=%fused_computation.11 | convolution fusion | flops 536870912 | bytes 10551296 | tf_op jit(solution)/shard_map/rihc,rjc->rhij/dot_general | solution.py:116
  106.9 5.8 %fusion.97 = (f32[128,64]{1,0:T(8,128)S(1)}, f32[1,128,64,64]{2,3,1,0:T(8,128)}) fusion(f32[64,128,64]{0,2,1:T(8,128)S(1)} %fusion.10, bf16[1,64,64]{2,1,0:T(8,128)(2,1)S(1)} %copy-done.8, bf16[1,64,128,576]{3,1,0,2:T(8,128)(2,1)} %all-gather.10.cloned.1.call-done, pred[64,64]{0,1:T(8,128)(4,1)S(1)} %copy.45), kind=kOutput, calls=%fused_computation.169 | convolution fusion | flops 69197824 | bytes 6336512 | tf_op jit(solution)/shard_map/rihe,rje->rhij/dot_general | solution.py:119
  112.8 7.7 %split.8 = bf16[1,64,128,512]{3,1,0,2:T(8,128)(2,1)} slice(bf16[1,64,128,576]{3,1,0,2:T(8,128)(2,1)} %all-gather.10.cloned.1.call-done), slice={[0:1], [0:64], [0:128], [0:512]} | slice | bytes 16777216 | tf_op jit(solution)/shard_map/split | solution.py:22
  120.5 30.0 %fusion.12 = f32[64,128,1024]{2,1,0:T(8,128)} fusion(bf16[1,64,128,512]{3,1,0,2:T(8,128)(2,1)} %split.8, bf16[1,1024,512]{2,1,0:T(8,128)(2,1)S(1)} %copy-done), kind=kOutput, calls=%fused_computation.14 | convolution fusion | flops 8589934592 | bytes 42991616 | tf_op jit(solution)/shard_map/rihc,rtc->rhit/dot_general | solution.py:107
  150.5 21.9 %fusion.96 = (f32[128,64]{0,1:T(8,128)S(1)}, f32[1,128,64,1024]{3,1,2,0:T(8,128)}) fusion(f32[64,128,1024]{2,1,0:T(8,128)} %fusion.12, bf16[1,1024,64]{1,2,0:T(8,128)(2,1)S(1)} %copy-done.4, bf16[1,64,128,64]{2,3,1,0:T(8,128)(2,1)S(1)} %copy-done.3, pred[1024]{0:T(1024)(128)(4,1)S(1)} %add_compare_fusion), kind=kOutput, calls=%fused_computation.168 | convolution fusion | flops 1107288064 | bytes 68322304 | tf_op jit(solution)/shard_map/rihe,rte->rhit/dot_general | solution.py:110
  172.5 15.1 %all_to_all.10 = f32[16,1,128,64]{2,3,1,0:T(8,128)S(1)} all-to-all(f32[16,1,128,64]{2,3,1,0:T(8,128)S(1)} %broadcast_in_dim.37), channel_id=1, replica_groups=mesh['seq_0'=4,'seq_1'=4,'batch_0'=4,'batch_1'=2] {'seq_0','seq_1'}, dimensions={0} | all-to-all | bytes 1048576 | tf_op jit(solution)/shard_map/all_to_all | solution.py:27
  187.7 18.7 %fusion.7 = f32[1,128,64,512]{3,1,2,0:T(8,128)} fusion(f32[1,128,64,1024]{3,1,2,0:T(8,128)} %get-tuple-element.19, f32[128,64]{0,1:T(8,128)S(1)} %reduce_max.38, bf16[1,1024,512]{2,1,0:T(8,128)(2,1)S(1)} %copy-done), kind=kOutput, calls=%fused_computation.10 | convolution fusion | flops 8606711808 | bytes 51412992 | tf_op jit(solution)/shard_map/rhit,rtc->rhic/dot_general | solution.py:129
  206.5 0.6 copy-done.12
  207.0 0.6 dynamic-slice.5
  208.3 0.1 constant_dynamic-slice_fusion.1
  208.4 1.0 fusion.24
  209.4 0.1 copy.67
  209.5 14.9 %fusion.1 = f32[128,64]{0,1:T(8,128)S(1)} fusion(f32[1,128,64,1024]{3,1,2,0:T(8,128)} %get-tuple-element.19, f32[128,64]{0,1:T(8,128)S(1)} %reduce_max.38), kind=kLoop, calls=%fused_computation.5 | loop fusion | flops 16769024 | bytes 33619968 | tf_op jit(solution)/shard_map/reduce_sum | solution.py:128
  224.5 0.1 copy.53
  224.6 58.5 %all-reduce = f32[1,128,64]{2,1,0:T(8,128)S(1)} all-reduce(f32[1,128,64]{2,1,0:T(8,128)S(1)} %copy.53), channel_id=7, replica_groups=mesh['seq_0'=4,'seq_1'=4,'batch_0'=4,'batch_1'=2] {'seq_0','seq_1'}, use_global_device_ids=true, to_apply=%region_5.6.clone | all-reduce | flops 8192 | bytes 65536
  283.1 0.1 copy.55
  283.2 0.1 copy.61
  283.4 34.0 %reduce-scatter.3.cloned.1.call-done = f32[1,8,64,512]{3,1,2,0:T(8,128)} async-done(((f32[1,128,64,512]{3,1,2,0:T(8,128)}), f32[1,8,64,512]{3,1,2,0:T(8,128)}) %reduce-scatter.3.cloned.1.call-update) | async-done | bytes 1048592 | tf_op jit(solution)/shard_map/reduce_scatter | solution.py:146
  317.4 1.5 fusion.15
  318.9 0.4 fusion.19
  319.3 0.1 copy.57
  319.4 7.9 %fusion.27 = f32[64,7168]{1,0:T(8,128)S(1)} fusion(bf16[1024,7168]{1,0:T(8,128)(2,1)} %param.25, bf16[8,8,8,128]{3,2,1,0:T(8,128)(2,1)S(1)} %bitcast.378), kind=kOutput, calls=%fused_computation.45 | convolution fusion | flops 939524096 | bytes 16646144 | tf_op jit(solution)/shard_map/dot_general | solution.py:157
  327.3 0.1 convert_add_fusion
  327.4 1.1 add.352
  328.5 1.2 copy-done.2
  329.8 88.1 %all-reduce.3.cloned.1.call-done = f32[64,7168]{1,0:T(8,128)} async-done(((f32[64,7168]{1,0:T(8,128)}), f32[64,7168]{1,0:T(8,128)}) %all-reduce.3.cloned.1.call-update) | async-done | bytes 1835024 | tf_op jit(solution)/shard_map/psum | solution.py:163
  417.9 1.7 multiply_reduce_fusion
  419.7 1.7 multiply_convert_fusion
  421.4 3.9 stack.2
  425.3 6.9 %all-to-all-start.1 = ((bf16[8,64,7168]{2,1,0:T(8,128)(2,1)}), bf16[8,64,7168]{2,1,0:T(8,128)(2,1)}, u32[]{:S(2)}, u32[]{:S(2)}) async-start(bf16[8,64,7168]{2,1,0:T(8,128)(2,1)} %stack.2), calls=%async_computation.2 | async-start | bytes 14680064 | tf_op jit(solution)/shard_map/all_to_all | solution.py:176
  433.0 0.1 reshape.1092
  433.1 1.6 dynamic-slice_convert_fusion
  434.7 80.1 %all-to-all-done.1 = bf16[8,64,7168]{2,1,0:T(8,128)(2,1)} async-done(((bf16[8,64,7168]{2,1,0:T(8,128)(2,1)}), bf16[8,64,7168]{2,1,0:T(8,128)(2,1)}, u32[]{:S(2)}, u32[]{:S(2)}) %all-to-all-start.1) | async-done | bytes 7340064 | tf_op jit(solution)/shard_map/all_to_all | solution.py:176
  514.8 8.5 %fusion.98 = (f32[512]{0:T(512)S(1)}, f32[512,512]{0,1:T(8,128)S(1)}) fusion(bf16[512,7168]{1,0:T(8,128)(2,1)} %bitcast.35, bf16[512,7168]{1,0:T(8,128)(2,1)} %param.27), kind=kOutput, calls=%fused_computation.170 | convolution fusion | flops 3758358016 | bytes 15730688 | tf_op jit(solution)/shard_map/rd,vd->rv/dot_general | solution.py:173
  523.4 0.3 copy.58
  523.7 0.2 exponential_reduce_fusion
  523.9 1.6 gather_fusion
  525.5 0.3 select_reduce_fusion
  525.8 9.0 %all-gather.4 = f32[4,3,512]{2,1,0:T(4,128)S(1)} all-gather(f32[1,3,512]{2,1,0:T(4,128)S(1)} %maximum_bitcast_fusion.1), channel_id=2, replica_groups=mesh['seq_0'=4,'seq_1'=4,'batch_0'=4,'batch_1'=2] {'seq_0'}, dimensions={0}, use_global_device_ids=true | all-gather | bytes 30720 | tf_op jit(solution)/shard_map/all_gather | solution.py:43
  534.9 9.0 %all-gather.5 = f32[4,3,512]{2,1,0:T(4,128)S(1)} all-gather(f32[1,3,512]{2,1,0:T(4,128)S(1)} %maximum_bitcast_fusion.2), channel_id=3, replica_groups=mesh['seq_0'=4,'seq_1'=4,'batch_0'=4,'batch_1'=2] {'seq_1'}, dimensions={0}, use_global_device_ids=true | all-gather | bytes 30720 | tf_op jit(solution)/shard_map/all_gather | solution.py:43
  544.0 9.0 %all-gather.6 = f32[4,3,512]{2,1,0:T(4,128)S(1)} all-gather(f32[1,3,512]{2,1,0:T(4,128)S(1)} %maximum_bitcast_fusion.3), channel_id=4, replica_groups=mesh['seq_0'=4,'seq_1'=4,'batch_0'=4,'batch_1'=2] {'batch_0'}, dimensions={0}, use_global_device_ids=true | all-gather | bytes 30720 | tf_op jit(solution)/shard_map/all_gather | solution.py:43
  553.1 11.0 %all-gather.7 = f32[2,3,512]{2,1,0:T(4,128)S(1)} all-gather(f32[1,3,512]{2,1,0:T(4,128)S(1)} %maximum_bitcast_fusion.4), channel_id=5, replica_groups=mesh['seq_0'=4,'seq_1'=4,'batch_0'=4,'batch_1'=2] {'batch_1'}, dimensions={0}, use_global_device_ids=true | all-gather | bytes 18432 | tf_op jit(solution)/shard_map/all_gather | solution.py:43
  564.1 3.5 gather_fusion.1
  567.6 0.1 gather.10
  567.8 1.1 fusion.89
  (61 shorter events, 1.0 us)
Async XLA Ops:
  7.2 113.3 %copy-start = (bf16[1,1024,512]{2,1,0:T(8,128)(2,1)S(1)}, bf16[1,1024,512]{2,1,0:T(8,128)(2,1)}, u32[]{:S(2)}) copy-start(bf16[1,1024,512]{2,1,0:T(8,128)(2,1)} %param.20) | copy-start | bytes 3145732
  7.2 92.3 %copy-start.5 = (bf16[1,64,512]{2,1,0:T(8,128)(2,1)S(1)}, bf16[1,64,512]{2,1,0:T(8,128)(2,1)}, u32[]{:S(2)}) copy-start(bf16[1,64,512]{2,1,0:T(8,128)(2,1)} %param.22) | copy-start | bytes 196612
  7.2 87.5 %all-gather.10.cloned.1.call-start = ((), (), s32[]{:S(2)}) async-start(), calls=%async_computation.3 | async-start | bytes 11141120 | tf_op jit(solution)/shard_map/all_gather | solution.py:22
  10.8 306.6 %reduce-scatter.3.cloned.1.call-start = ((), (), s32[]{:S(2)}) async-start(), calls=%async_computation.4 | async-start | bytes 17825792 | tf_op jit(solution)/shard_map/reduce_scatter | solution.py:146
  96.5 10.4 %copy-start.8 = (bf16[1,64,64]{2,1,0:T(8,128)(2,1)S(1)}, bf16[1,64,64]{2,1,0:T(8,128)(2,1)}, u32[]{:S(2)}) copy-start(bf16[1,64,64]{2,1,0:T(8,128)(2,1)} %param.23) | copy-start | bytes 24580
  120.5 30.0 %copy-start.3 = (bf16[1,64,128,64]{2,3,1,0:T(8,128)(2,1)S(1)}, bf16[1,64,128,64]{2,3,1,0:T(8,128)(2,1)}, u32[]{:S(2)}) copy-start(bf16[1,64,128,64]{2,3,1,0:T(8,128)(2,1)} %copy.69) | copy-start | bytes 3145732
  120.5 30.0 %copy-start.4 = (bf16[1,1024,64]{1,2,0:T(8,128)(2,1)S(1)}, bf16[1,1024,64]{1,2,0:T(8,128)(2,1)}, u32[]{:S(2)}) copy-start(bf16[1,1024,64]{1,2,0:T(8,128)(2,1)} %param.21) | copy-start | bytes 393220
  206.4 0.7 copy-start.12
  206.4 211.5 %all-reduce.3.cloned.1.call-start = ((), (), s32[]{:S(2)}) async-start(), calls=%async_computation.5 | async-start | bytes 3670016 | tf_op jit(solution)/shard_map/psum | solution.py:163
  209.5 109.4 %copy-start.11 = (bf16[8,512,128]{2,1,0:T(8,128)(2,1)S(1)}, bf16[8,512,128]{2,1,0:T(8,128)(2,1)}, u32[]{:S(2)}) copy-start(bf16[8,512,128]{2,1,0:T(8,128)(2,1)} %param.19) | copy-start | bytes 3145732
  319.4 7.9 %copy-start.6 = (bf16[64,448]{1,0:T(8,128)(2,1)S(1)}, bf16[64,448]{1,0:T(8,128)(2,1)}, u32[]{:S(2)}) copy-start(bf16[64,448]{1,0:T(8,128)(2,1)} %param.24) | copy-start | bytes 172036
  319.4 100.2 %copy-start.7 = (f32[7168]{0:T(1024)S(1)}, f32[7168]{0:T(1024)}, u32[]{:S(2)}) copy-start(f32[7168]{0:T(1024)} %param.26) | copy-start | bytes 86020
  328.5 1.3 copy-start.2
  425.3 7.5 %copy-start.9 = (s32[8,64]{1,0:T(8,128)S(1)}, s32[8,64]{1,0:T(8,128)}, u32[]{:S(2)}) copy-start(s32[8,64]{1,0:T(8,128)} %param.29) | copy-start | bytes 6148
  425.3 7.6 %copy-start.10 = (s32[8,64]{1,0:T(8,128)S(1)}, s32[8,64]{1,0:T(8,128)}, u32[]{:S(2)}) copy-start(s32[8,64]{1,0:T(8,128)} %param.28) | copy-start | bytes 6148
  425.3 89.5 %all-to-all-start.1 = ((bf16[8,64,7168]{2,1,0:T(8,128)(2,1)}), bf16[8,64,7168]{2,1,0:T(8,128)(2,1)}, u32[]{:S(2)}, u32[]{:S(2)}) async-start(bf16[8,64,7168]{2,1,0:T(8,128)(2,1)} %stack.2), calls=%async_computation.2 | async-start | bytes 14680064 | tf_op jit(solution)/shard_map/all_to_all | solution.py:176
  514.8 54.1 %copy-start.1 = (bf16[1,1024,512]{2,1,0:T(8,128)(2,1)S(1)}, bf16[1,1024,512]{2,1,0:T(8,128)(2,1)}, u32[]{:S(2)}) copy-start(bf16[1,1024,512]{2,1,0:T(8,128)(2,1)} %param.20) | copy-start | bytes 3145732
Sparse Core Ops, SparseCore 0:
  10.9 83.7 all-gather.9
  206.5 110.8 reduce-scatter.2
  329.9 87.9 all-reduce.2
